TPU v7x, 256 devices: a whole 4x4x8 slice. The times are simulated.
256 devices in a mesh: seq: 16 (over z, x_lo), db: 16 (over x_hi, y, core).
Axes of the slice: x: 4 (x_hi: 2, x_lo: 2; x = x_hi * 2 + x_lo), y: 4, z: 8, core: 2. Of those that a mesh axis runs over, the one named last changes fastest.
Arguments:
- decoder_states: bfloat16 [16384, 4096], P('seq'), may hold values from -6 to 6
- query_weight: bfloat16 [4096, 4096], P(None, 'db'), may hold values from -0.09375 to 0.09375
- output_weight: bfloat16 [4096, 4096], P('db'), may hold values from -0.5 to 0.5
- neighbour_kv: bfloat16 [128, 128, 2, 4096], P('seq', None, None, 'db'), may hold values from -110 to 110
- neighbour_shard: int32 [256, 2], P('seq'), may hold values from 0 to 15, all different within a row; in each aligned block of 16 rows (0 to 15, 16 to 31, ...) at most 3 rows name the same one
- neighbour_entry: int32 [256, 2], P('seq'), may hold values from 0 to 7
- neighbour_count: int32 [256], P('seq'), may hold values from 1 to 2
Outputs:
- cross_out: bfloat16 [16384, 4096], P('seq', 'db')
Inputs may be any that keep to these rules, and one draw needn't show every extreme that they name: `neighbour_shard`: in each aligned block of 16 spans (the spans of one index of seq), no shard is named by more than 3 spans and one shard is named by exactly 3; the 2 neighbours of one span lie on different shards.
All inputs are finite; a program needn't handle non-finite values.
Results may differ from a plain program's by a relative error of at most 0.017.
Values may be sent and summed in bfloat16 or wider, within the bound.
A program may use at most 128 MiB of HBM per device.

v0:
```python
import math
import jax
import jax.numpy as jnp
from jax import lax
from jax.sharding import PartitionSpec as P

HD = 128
SPAN = 64
K = 2


def on_device(
    decoder_states,
    query_weight,
    output_weight,
    neighbour_kv,
    neighbour_shard,
    neighbour_entry,
    neighbour_count,
):
    tok_rows = decoder_states.shape[0]
    span_total = tok_rows // SPAN
    row_width = query_weight.shape[1]
    heads_here = row_width // HD
    ent_dev = neighbour_kv.shape[0]
    key_len = neighbour_kv.shape[1]
    queries = jnp.dot(decoder_states, query_weight, preferred_element_type=jnp.float32).astype(
        jnp.bfloat16
    )
    queries = queries.reshape(span_total, SPAN, heads_here, HD)
    owners = neighbour_shard.reshape(-1)
    entries = neighbour_entry.reshape(-1)
    item_count = owners.shape[0]
    empty_blocks = jnp.zeros((item_count,) + neighbour_kv.shape[1:], jnp.bfloat16)
    shard_rows = lax.all_gather(neighbour_kv, "seq", axis=0, tiled=True)
    shard_len = shard_rows.shape[0]
    local_idx = owners * ent_dev + entries
    inside = (local_idx >= 0) & (local_idx < shard_len)
    taken_rows = jnp.take(shard_rows, jnp.clip(local_idx, 0, shard_len - 1), axis=0)
    blocks = jnp.where(inside[:, None, None, None], taken_rows, empty_blocks)
    blocks = blocks.reshape(span_total, K, key_len, 2, heads_here, HD)
    key_rows = blocks[:, :, :, 0]
    val_rows = blocks[:, :, :, 1]
    scores = jnp.einsum(
        "cqhd,cknhd->chqkn", queries, key_rows, preferred_element_type=jnp.float32
    ) * (1.0 / math.sqrt(HD))
    live_slots = jnp.arange(K, dtype=jnp.int32)[None, :] < neighbour_count[:, None]
    masked = live_slots[:, None, None, :, None]
    scores = jnp.where(masked, scores, -1e30)
    top_score = jnp.max(scores, axis=(3, 4), keepdims=True)
    exponent = jnp.where(masked, jnp.exp(scores - top_score), 0.0)
    probs_bf = (exponent / jnp.sum(exponent, axis=(3, 4), keepdims=True)).astype(jnp.bfloat16)
    context = jnp.einsum(
        "chqkn,cknhd->cqhd", probs_bf, val_rows, preferred_element_type=jnp.float32
    )
    context = context.astype(jnp.bfloat16).reshape(tok_rows, row_width)
    partial_value = jnp.dot(context, output_weight, preferred_element_type=jnp.float32)
    return lax.psum_scatter(
        partial_value.astype(jnp.bfloat16), "db", scatter_dimension=1, tiled=True
    )


def solution(mesh):
    in_specs = (
        P("seq", None),
        P(None, "db"),
        P("db", None),
        P("seq", None, None, "db"),
        P("seq", None),
        P("seq", None),
        P("seq"),
    )
    out_specs = P("seq", "db")
    return jax.shard_map(
        on_device, mesh=mesh, in_specs=in_specs, out_specs=out_specs, check_vma=False
    )
```

profile of v0, /device:TPU:1, one launch (start us, length us, event | category | flops | bytes accessed | tf_op | source)
XLA Modules:
  0.0 518.9 jit_solution(15466624254692914322)
XLA Ops:
  6.5 0.0 copy-start
  6.5 0.0 copy-start.2
  6.5 0.0 copy-start.1
  6.5 0.0 all-gather.2.cloned.1.call-start
  6.5 2.5 copy.28
  9.1 0.0 all-gather.2.cloned.1.call-update
  9.1 0.0 reduce-scatter.2.cloned.1.call-start
  9.1 0.0 copy-done.2
  9.1 0.0 copy-done.1
  9.2 0.1 copy.29
  9.3 0.1 min.12
  9.3 0.1 copy.26
  9.4 0.1 copy.27
  9.5 0.0 copy-start.3
  9.5 6.3 %convolution_convert_fusion.1 = bf16[1024,256]{1,0:T(8,128)(2,1)S(1)} fusion(bf16[1024,4096]{1,0:T(8,128)(2,1)} %param.7, bf16[4096,256]{1,0:T(8,128)(2,1)} %param.8), kind=kOutput, calls=%fused_computation.13 | convolution fusion | flops 2147745792 | bytes 11010048 | tf_op jit(solution)/shard_map/dot_general | solution.py:27
  15.9 0.1 reshape.92
  16.0 0.0 copy-done.3
  16.0 0.1 iota_compare_fusion
  16.1 347.9 %all-gather.2.cloned.1.call-done = bf16[128,128,2,256]{3,1,2,0:T(8,128)(2,1)} async-done(((bf16[8,128,2,256]{3,1,2,0:T(8,128)(2,1)}), bf16[128,128,2,256]{3,1,2,0:T(8,128)(2,1)}) %all-gather.2.cloned.1.call-update) | async-done | bytes 16777232 | tf_op jit(solution)/shard_map/all_gather | solution.py:35
  364.0 8.5 %gather_fusion = bf16[32,128,2,256]{3,1,2,0:T(8,128)(2,1)} fusion(bf16[128,128,2,256]{3,1,2,0:T(8,128)(2,1)} %all-gather.2.cloned.1.call-done, s32[1024]{0:T(1024)S(1)} %pad_clamp_fusion), kind=kCustom, calls=%fused_computation | custom fusion | bytes 8388736 | tf_op jit(solution)/shard_map/jit(_take)/gather | solution.py:39
  372.5 6.5 %copy.30 = bf16[32,128,2,256]{1,3,2,0:T(8,128)(2,1)} copy(bf16[32,128,2,256]{3,1,2,0:T(8,128)(2,1)} %gather_fusion) | data formatting | bytes 8388608 | tf_op jit(solution)/shard_map/jit(_take)/gather | solution.py:39
  379.0 6.2 %copy.31 = bf16[16,2,128,2,2,128]{5,2,1,4,0,3:T(8,128)(2,1)} copy(bf16[16,2,128,2,2,128]{2,5,4,3,1,0:T(8,128)(2,1)} %bitcast.35) | data formatting | bytes 8388608 | tf_op jit(solution)/shard_map/jit(_take)/gather | solution.py:39
  385.2 2.9 select_select_fusion
  388.1 1.0 fusion.2
  389.1 1.2 fusion.3
  390.3 1.1 fusion.6
  391.4 0.5 copy.33
  391.9 0.0 copy-done
  391.9 5.6 %convolution_convert_fusion = bf16[1024,4096]{1,0:T(8,128)(2,1)} fusion(bf16[256,4096]{1,0:T(8,128)(2,1)S(1)} %copy-done, bf16[128,8,2,128]{3,2,1,0:T(2,128)(2,1)S(1)} %bitcast.36), kind=kOutput, calls=%fused_computation.1 | convolution fusion | flops 2151677952 | bytes 11010048 | tf_op jit(solution)/shard_map/dot_general | solution.py:57
  397.5 0.0 reduce-scatter.2.cloned.1.call-update
  397.5 114.5 %reduce-scatter.2.cloned.1.call-done = bf16[1024,256]{1,0:T(8,128)(2,1)} async-done(((bf16[1024,4096]{1,0:T(8,128)(2,1)}), bf16[1024,256]{1,0:T(8,128)(2,1)}) %reduce-scatter.2.cloned.1.call-update) | async-done | bytes 524304 | tf_op jit(solution)/shard_map/reduce_scatter | solution.py:58
  (3 shorter events, 0.0 us)
Async XLA Ops:
  6.5 385.4 %copy-start = (bf16[256,4096]{1,0:T(8,128)(2,1)S(1)}, bf16[256,4096]{1,0:T(8,128)(2,1)}, u32[]{:S(2)}) copy-start(bf16[256,4096]{1,0:T(8,128)(2,1)} %param.9) | copy-start | bytes 6291460
  6.5 2.6 copy-start.2
  6.5 2.6 copy-start.1
  6.5 357.5 %all-gather.2.cloned.1.call-start = ((), (), s32[]{:S(2)}) async-start(), calls=%async_computation.1 | async-start | bytes 17825792 | tf_op jit(solution)/shard_map/all_gather | solution.py:35
  9.1 502.9 %reduce-scatter.2.cloned.1.call-start = ((), (), s32[]{:S(2)}) async-start(), calls=%async_computation.2 | async-start | bytes 8912896 | tf_op jit(solution)/shard_map/reduce_scatter | solution.py:58
  9.5 6.5 %copy-start.3 = (s32[16]{0:T(128)S(1)}, s32[16]{0:T(128)}, u32[]{:S(2)}) copy-start(s32[16]{0:T(128)} %param.13) | copy-start | bytes 196
Sparse Core Ops, SparseCore 0:
  9.2 354.7 all-gather.1
  397.6 114.3 reduce-scatter.1
where the time goes:
time: 519 us
  waiting for transfers between devices  462 us (89%)
  local copies, waits for them, and re-layouts  24.8 us (5%)
  matrix products  13.9 us (3%)
  between operations  13.5 us (3%)
    all_gather x1, waiting for transfers between devices, on_device(): shard_rows = lax.all_gather(neighbour_kv, 'seq', axis=0, tiled=True)  348 us
    reduce_scatter x1, waiting for transfers between devices, on_device(): lax.psum_scatter(partial_value.astype(jnp.bfloat16), 'db', scatter_dimens...  114 us
    gather x3, local copies, waits for them, and re-layouts, on_device(): jnp.take(shard_rows, jnp.clip(local_idx, 0, shard_len - 1), axis=0)  21.2 us
  transfers between devices with their start and end apart: 2, of which 2 were waited for; matrix products, arithmetic and copies ran while one was open for 1% of the time, Pallas kernels for 0%

commit v1 on v0

--- a/solution.py
+++ b/solution.py
@@ -32,7 +32,8 @@
     entries = neighbour_entry.reshape(-1)
     item_count = owners.shape[0]
     empty_blocks = jnp.zeros((item_count,) + neighbour_kv.shape[1:], jnp.bfloat16)
-    shard_rows = lax.all_gather(neighbour_kv, "seq", axis=0, tiled=True)
+    sent = jnp.stack([neighbour_kv] * lax.axis_size("seq"))
+    shard_rows = jnp.concatenate(lax.all_to_all(sent, "seq", 0, 0), axis=0)
     shard_len = shard_rows.shape[0]
     local_idx = owners * ent_dev + entries
     inside = (local_idx >= 0) & (local_idx < shard_len)

time: 519 us -> 557 us (1.073)
  waiting for transfers between devices: 462 us -> 485 us
  starting transfers between devices: 0.04 us -> 10.3 us
    all_to_all x0 -> x1, waiting for transfers between devices: none -> 375 us  [on_device(): shard_rows = jnp.concatenate(lax.all_to_all(sent, 'seq', 0, 0), axis=0)]
    all_gather x1 -> x0, waiting for transfers between devices: 348 us -> none  [on_device(): shard_rows = lax.all_gather(neighbour_kv, 'seq', axis=0, tiled=True)]
    all_to_all x0 -> x1, starting transfers between devices: none -> 10.2 us  [on_device(): shard_rows = jnp.concatenate(lax.all_to_all(sent, 'seq', 0, 0), axis=0)]
    another operation x0 -> x1, local copies, waits for them, and re-layouts: none -> 5.98 us  [on_device(): sent = jnp.stack([neighbour_kv] * lax.axis_size('seq'))]
where the time goes in v1:
time: 557 us; the launch traced here: 556 us
  waiting for transfers between devices  485 us (87%)
  local copies, waits for them, and re-layouts  29.8 us (5%)
  matrix products  13.9 us (2%)
  between operations  13.5 us (2%)
  starting transfers between devices  10.3 us (2%)
    all_to_all x1, waiting for transfers between devices, on_device(): shard_rows = jnp.concatenate(lax.all_to_all(sent, 'seq', 0, 0), axis=0)  375 us
    reduce_scatter x1, waiting for transfers between devices, on_device(): lax.psum_scatter(partial_value.astype(jnp.bfloat16), 'db', scatter_dimens...  109 us
    gather x3, local copies, waits for them, and re-layouts, on_device(): jnp.take(shard_rows, jnp.clip(local_idx, 0, shard_len - 1), axis=0)  21.2 us
  transfers between devices with their start and end apart: 2, of which 2 were waited for; matrix products, arithmetic and copies ran while one was open for 1% of the time, Pallas kernels for 0%

profile of v1, /device:TPU:1, one launch (start us, length us, event | category | flops | bytes accessed | tf_op | source)
XLA Modules:
  0.0 556.3 jit_solution(2814450634607525181)
XLA Ops:
  6.5 0.0 copy-start
  6.5 1.5 copy.20
  8.1 6.0 %stack.2 = bf16[16,8,128,2,256]{4,2,3,1,0:T(8,128)(2,1)} broadcast(bf16[8,128,2,256]{3,1,2,0:T(8,128)(2,1)S(1)} %copy.20), dimensions={1,2,3,4} | broadcast | bytes 17825792 | tf_op jit(solution)/shard_map/stack | solution.py:35
  14.1 0.0 copy-start.1
  14.1 0.0 copy-start.2
  14.1 10.2 %all-to-all-start = ((bf16[16,8,128,2,256]{4,2,3,1,0:T(8,128)(2,1)}), bf16[16,8,128,2,256]{4,2,3,1,0:T(8,128)(2,1)}, u32[]{:S(2)}, u32[]{:S(2)}) async-start(bf16[16,8,128,2,256]{4,2,3,1,0:T(8,128)(2,1)} %stack.2), calls=%async_computation | async-start | bytes 33554432 | tf_op jit(solution)/shard_map/all_to_all | solution.py:36
  24.3 0.0 reduce-scatter.2.cloned.1.call-start
  24.4 0.0 copy-done.1
  24.4 0.0 copy-done.2
  24.4 0.1 copy.21
  24.5 0.1 min.12
  24.6 0.1 copy.19
  24.7 0.1 copy.18
  24.8 0.0 copy-start.3
  24.8 6.3 %convolution_convert_fusion.1 = bf16[1024,256]{1,0:T(8,128)(2,1)S(1)} fusion(bf16[1024,4096]{1,0:T(8,128)(2,1)} %param.7, bf16[4096,256]{1,0:T(8,128)(2,1)} %param.8), kind=kOutput, calls=%fused_computation.13 | convolution fusion | flops 2147745792 | bytes 11010048 | tf_op jit(solution)/shard_map/dot_general | solution.py:27
  31.1 0.1 reshape.98
  31.2 0.0 copy-done.3
  31.3 0.1 iota_compare_fusion
  31.3 375.5 %all-to-all-done = bf16[16,8,128,2,256]{4,2,3,1,0:T(8,128)(2,1)} async-done(((bf16[16,8,128,2,256]{4,2,3,1,0:T(8,128)(2,1)}), bf16[16,8,128,2,256]{4,2,3,1,0:T(8,128)(2,1)}, u32[]{:S(2)}, u32[]{:S(2)}) %all-to-all-start) | async-done | bytes 16777248 | tf_op jit(solution)/shard_map/all_to_all | solution.py:36
  406.8 8.5 %gather_fusion = bf16[32,128,2,256]{3,1,2,0:T(8,128)(2,1)} fusion(bf16[128,128,2,256]{3,1,2,0:T(8,128)(2,1)} %bitcast, s32[1024]{0:T(1024)S(1)} %pad_clamp_fusion), kind=kCustom, calls=%fused_computation | custom fusion | bytes 8388736 | tf_op jit(solution)/shard_map/jit(_take)/gather | solution.py:40
  415.3 6.5 %copy.22 = bf16[32,128,2,256]{1,3,2,0:T(8,128)(2,1)} copy(bf16[32,128,2,256]{3,1,2,0:T(8,128)(2,1)} %gather_fusion) | data formatting | bytes 8388608 | tf_op jit(solution)/shard_map/jit(_take)/gather | solution.py:40
  421.8 6.2 %copy.23 = bf16[16,2,128,2,2,128]{5,2,1,4,0,3:T(8,128)(2,1)} copy(bf16[16,2,128,2,2,128]{2,5,4,3,1,0:T(8,128)(2,1)} %bitcast.36) | data formatting | bytes 8388608 | tf_op jit(solution)/shard_map/jit(_take)/gather | solution.py:40
  428.0 2.9 select_select_fusion
  430.9 1.0 fusion.2
  431.9 1.2 fusion.3
  433.1 1.1 fusion.6
  434.2 0.5 copy.25
  434.7 0.0 copy-done
  434.7 5.6 %convolution_convert_fusion = bf16[1024,4096]{1,0:T(8,128)(2,1)} fusion(bf16[256,4096]{1,0:T(8,128)(2,1)S(1)} %copy-done, bf16[128,8,2,128]{3,2,1,0:T(2,128)(2,1)S(1)} %bitcast.37), kind=kOutput, calls=%fused_computation.1 | convolution fusion | flops 2151677952 | bytes 11010048 | tf_op jit(solution)/shard_map/dot_general | solution.py:58
  440.3 0.0 reduce-scatter.2.cloned.1.call-update
  440.3 109.1 %reduce-scatter.2.cloned.1.call-done = bf16[1024,256]{1,0:T(8,128)(2,1)} async-done(((bf16[1024,4096]{1,0:T(8,128)(2,1)}), bf16[1024,256]{1,0:T(8,128)(2,1)}) %reduce-scatter.2.cloned.1.call-update) | async-done | bytes 524304 | tf_op jit(solution)/shard_map/reduce_scatter | solution.py:59
  (3 shorter events, 0.0 us)
Async XLA Ops:
  6.5 428.2 %copy-start = (bf16[256,4096]{1,0:T(8,128)(2,1)S(1)}, bf16[256,4096]{1,0:T(8,128)(2,1)}, u32[]{:S(2)}) copy-start(bf16[256,4096]{1,0:T(8,128)(2,1)} %param.9) | copy-start | bytes 6291460
  14.1 10.3 %copy-start.1 = (s32[16,2]{0,1:T(2,128)S(1)}, s32[16,2]{0,1:T(2,128)}, u32[]{:S(2)}) copy-start(s32[16,2]{0,1:T(2,128)} %param.12) | copy-start | bytes 388
  14.1 10.3 %copy-start.2 = (s32[16,2]{0,1:T(2,128)S(1)}, s32[16,2]{0,1:T(2,128)}, u32[]{:S(2)}) copy-start(s32[16,2]{0,1:T(2,128)} %param.11) | copy-start | bytes 388
  14.1 392.7 %all-to-all-start = ((bf16[16,8,128,2,256]{4,2,3,1,0:T(8,128)(2,1)}), bf16[16,8,128,2,256]{4,2,3,1,0:T(8,128)(2,1)}, u32[]{:S(2)}, u32[]{:S(2)}) async-start(bf16[16,8,128,2,256]{4,2,3,1,0:T(8,128)(2,1)} %stack.2), calls=%async_computation | async-start | bytes 33554432 | tf_op jit(solution)/shard_map/all_to_all | solution.py:36
  24.3 525.1 %reduce-scatter.2.cloned.1.call-start = ((), (), s32[]{:S(2)}) async-start(), calls=%async_computation.2 | async-start | bytes 8912896 | tf_op jit(solution)/shard_map/reduce_scatter | solution.py:59
  24.8 6.5 %copy-start.3 = (s32[16]{0:T(128)S(1)}, s32[16]{0:T(128)}, u32[]{:S(2)}) copy-start(s32[16]{0:T(128)} %param.13) | copy-start | bytes 196
Sparse Core Ops, SparseCore 0:
  440.4 108.9 reduce-scatter.1
